TPU v7x, 32 devices: a whole 2x2x4 slice. The times are simulated.
32 devices in a mesh: basin: 2 (over y), tx: 4 (over z), ty: 2 (over core), ev: 2 (over x).
Axes of the slice: x: 2, y: 2, z: 4, core: 2. Of those that a mesh axis runs over, the one named last changes fastest.
Arguments:
- depth0: float32 [4, 8, 8, 8, 256], P(('basin', 'ev'), None, None, 'tx', 'ty'), parts along dimension 0, may hold values from 0.6 to 1.4
- momentum0: float32 [4, 2, 8, 8, 8, 256], P(('basin', 'ev'), None, None, None, 'tx', 'ty'), parts along dimension 0, may hold values from -2.5 to 2.5
- obs_weight: float32 [4, 8, 8, 8, 256], P(('basin', 'ev'), None, None, 'tx', 'ty'), parts along dimension 0, as said below
- wet_mask: int32 [4, 4, 8, 256], P(('basin', 'ev'), None, 'tx', 'ty'), parts along dimension 0, may hold values 0 or 1
- zone_id: int32 [16, 256], P(('basin', 'tx'), 'ty'), parts along dimension 0, may hold values from 0 to 31
- manning: float32 [64], P('basin'), parts along dimension 0, may hold values from 0.2 to 0.6
Outputs:
- adjoint_state: float32 [4, 3, 8, 8, 8, 256], P(('basin', 'ev'), None, None, None, 'tx', 'ty'), parts along dimension 0
- rough_grad: float32 [64], P('basin'), parts along dimension 0
There are 2 independent parts, one for each index of `basin`. A program takes and returns all parts, laid end to end along the dimension named above; each array names one. Nothing has to cross between parts.
Inputs may be any that keep to these rules, and one draw needn't show every extreme that they name: `wet_mask`: 1 where an element is wet in that section of that event, else 0. `obs_weight`: positive weights.
All inputs are finite; a program needn't handle non-finite values. No bound on the sum of `wet_mask` on one device may be relied on, other than what follows from the above.
Results may differ from a plain program's by a relative error of at most 0.00005.
Values sent between devices are 32-bit elements; how exact they have to be, the bound alone decides.
No kernel may reach another device: no remote copies, remote signals or barrier semaphores. Data moves between devices by JAX's collectives and lax.ppermute only.
A program may use at most 64 MiB of HBM per device.

v0:
```python
import functools

import jax
import jax.numpy as jnp
import numpy as np
from jax import lax
from jax.experimental import pallas as pl
from jax.experimental.pallas import tpu as pltpu
from jax.sharding import PartitionSpec as P


NP = 8
NODES = NP * NP
LANES = 128
HALO = 8
PENALTY_SPEED = 4.0
TIME_STEP = 0.0005
SPEED_FLOOR = 0.01
COEFS = (0.5 * TIME_STEP, 0.5 * TIME_STEP, TIME_STEP)
WEIGHTS = (TIME_STEP / 6.0, TIME_STEP / 3.0, TIME_STEP / 3.0, TIME_STEP / 6.0)
F32 = jnp.float32
BF16 = jnp.bfloat16


def node_tables():
    points = -np.cos(np.pi * np.arange(NP) / (NP - 1))
    identity = np.eye(NP)
    differ = points[:, None] - points[None, :] + identity
    barycentric = 1.0 / np.prod(differ, axis=1)
    derivative = barycentric[None, :] / barycentric[:, None] / differ * (1.0 - identity)
    derivative = derivative - identity * derivative.sum(axis=1)[:, None]
    order = NP - 1
    end_weight = 1.0 / (order * order)
    return (derivative, float(1.0 / end_weight))


def split_table(main, ends):
    main = np.asarray(main, np.float32)
    high = main.astype(BF16)
    low = (main - high.astype(np.float32)).astype(BF16)
    ends = ends.astype(BF16)
    return np.concatenate([high, high, low, ends, ends], axis=1)


def split_data(main, ends):
    halves = []
    for blocks in (main, ends):
        data = jnp.concatenate(blocks, axis=0)
        high = data.astype(BF16)
        halves.append((high, (data - high.astype(F32)).astype(BF16)))
    (high, low), (end_high, end_low) = halves
    return jnp.concatenate([high, low, high, end_high, end_low], axis=0)


class Plan:
    def __init__(self, parts, cols, rows):
        self.parts = parts
        self.cols = cols
        self.width = rows // parts
        assert rows == LANES and parts * self.width == rows and self.width >= HALO
        self.window = self.width + 2 * HALO
        full, rest = divmod(self.window, self.width)
        self.segments = []
        tile = 0
        for column in range(cols):
            for piece in range(full):
                self.segments.append((tile, column, piece * self.width, self.width, 0))
                tile += 1
        if rest:
            per_tile = self.width // rest
            assert per_tile * rest == self.width
            for column in range(cols):
                self.segments.append(
                    (tile + column // per_tile, column, full * self.width, rest, column % per_tile * rest)
                )
            tile += -(-cols // per_tile)
        self.tiles = tile

    def find(self, column, row):
        for seg in self.segments:
            if seg[1] == column and seg[2] <= row < seg[2] + seg[3]:
                return seg
        return None

    def moves(self, side):
        table = [[] for _ in range(self.tiles)]
        for tile, column, first, count, offset in self.segments:
            if side in ("west", "east"):
                step = -1 if side == "west" else 1
                other = column + step
                wrap = 0
                if other < 0 or other >= self.cols:
                    wrap = step
                    other -= step * self.cols
                src = self.find(other, first)
                table[tile].append((src[0], src[4] - offset + wrap * self.width, offset, offset + count))
            else:
                step = -1 if side == "south" else 1
                table[tile].append((tile, step, offset, offset + count))
                edge = first - 1 if side == "south" else first + count
                src = self.find(column, edge)
                if src is not None:
                    at = offset if side == "south" else offset + count - 1
                    src_at = src[4] + edge - src[2]
                    table[tile].append((src[0], src_at - at, at, at + 1))
        merged = []
        for entries in table:
            kept = []
            for entry in entries:
                if kept and kept[-1][:2] == entry[:2] and kept[-1][3] == entry[2]:
                    kept[-1] = entry[:2] + (kept[-1][2], entry[3])
                else:
                    kept.append(entry)
            merged.append(kept)
        return merged


def roll(x, shift):
    shift = shift % LANES
    return x if shift == 0 else pltpu.roll(x, shift, 1)


def lane_iota(rows=8):
    return lax.broadcasted_iota(jnp.int32, (rows, LANES), 1)


def shifted(tiles, moves, offset_of):
    out = []
    for entries in moves:
        value = None
        for src, distance, first, end in entries:
            moved = roll(tiles[src], -distance)
            if value is None:
                value = moved
            else:
                value = jnp.where((offset_of >= first) & (offset_of < end), moved, value)
        out.append(value)
    return out


def exchange_out(pieces, put, me, parts, width):
    slot = lane_iota() // width
    for group in range(-(-len(pieces) // parts)):
        turned = []
        for j in range(parts):
            n = group * parts + j
            turned.append(roll(pieces[n](), width * j) if n < len(pieces) else None)
        for m in range(parts):
            dest = me ^ m
            turn = (slot - dest) & (parts - 1)
            value = turned[0]
            for j in range(1, parts):
                if turned[j] is not None:
                    value = jnp.where(turn == j, turned[j], value)
            put(m, group, value)


def exchange_in(get, count, me, parts, width):
    slot = lane_iota() // width
    for group in range(-(-count // parts)):
        turned = []
        for m in range(parts):
            source = me ^ m
            value = get(m, group)
            if m:
                value = pltpu.roll(value, ((source - me) & (parts - 1)) * width, 1)
            turned.append((source, value))
        for j in range(parts):
            n = group * parts + j
            if n < count:
                from_slot = (slot - j) & (parts - 1)
                value = turned[0][1]
                for source, other in turned[1:]:
                    value = jnp.where(from_slot == source, other, value)
                yield n, roll(value, -width * j)


def source_vreg(refs, array, i, column, cols):
    depth, momentum, weight, wet, zone = refs
    if array == 4:
        parts = [wet[0, :, column, :].astype(F32), zone[column : column + 1, :].astype(F32)]
        return jnp.concatenate(parts + [jnp.zeros((3, LANES), F32)], axis=0)
    ref = (depth, momentum, momentum, weight)[array]
    index = i + (NP if array == 2 else 0)
    return ref[index, pl.ds(column, NP, stride=cols), :]


SOURCES = [(array, i) for array in range(4) for i in range(NP)] + [(4, 0)]
PER_VREG = LANES // HALO


def chunks(count):
    size = NP // 2
    return [pl.ds(k, size) for k in range(0, count, size)] if count % size == 0 else [pl.ds(0, count)]


def halo_kernel(cols, *refs):
    sources, (copies, out, sems) = refs[:6], (refs[6:12], refs[12], refs[13])
    moves = []
    for src, dst in zip(sources, copies):
        for rows in chunks(src.shape[0]):
            moves.append(pltpu.make_async_copy(src.at[rows], dst.at[rows], sems.at[len(moves)]))
    for move in moves:
        move.start()
    for move in moves:
        move.wait()
    first = lax.axis_index("ty") == 0
    base = jnp.where(first, HALO, 0)
    slot = lane_iota() // HALO
    count = len(SOURCES) * cols
    for group in range(-(-count // PER_VREG)):
        value = jnp.zeros((8, LANES), F32)
        for k in range(PER_VREG):
            n = group * PER_VREG + k
            if n < count:
                (array, i), column = SOURCES[n // cols], n % cols
                moved = pltpu.roll(
                    source_vreg(copies[:5], array, i, column, cols), (base + HALO * k) & (LANES - 1), 1
                )
                value = jnp.where(slot == k, moved, value)
        out[group] = value


def turn_kernel(plan, depth, momentum, weight, wet, zone, out):
    refs = (depth, momentum, weight, wet, zone)
    offset_of = lane_iota() & (plan.width - 1)
    for number, (array, i) in enumerate(SOURCES):
        columns = [source_vreg(refs, array, i, column, plan.cols) for column in range(plan.cols)]
        for tile in range(plan.tiles):
            piece = number * plan.tiles + tile
            turn = plan.width * (piece % plan.parts)
            value = None
            for seg_tile, column, first, count, offset in plan.segments:
                if seg_tile == tile:
                    own = roll(columns[column], turn + offset - (first - HALO))
                    if value is None:
                        value = own
                    else:
                        at = (offset_of >= offset) & (offset_of < offset + count)
                        value = jnp.where(at, own, value)
            out[piece] = value


def pack_kernel(plan, turned, halo, *outs):
    me = lax.axis_index("tx")
    lane = lane_iota()
    cols, width, parts = plan.cols, plan.width, plan.parts
    slot = lane // width
    pieces = turned.shape[0]

    def within(start, length):
        return ((lane - start) & (LANES - 1)) < length

    def piece_with_halo(piece):
        number, tile = piece // plan.tiles, piece % plan.tiles
        turn = width * (piece % parts)
        value = turned[piece]
        for seg_tile, column, first, count, offset in plan.segments:
            if seg_tile != tile:
                continue
            n = number * cols + column
            remote, at = halo[n // PER_VREG], HALO * (n % PER_VREG)
            if first < HALO:
                start = (turn + offset) % LANES
                value = jnp.where(within(start, HALO - first), roll(remote, start - at - first), value)
            if first + count > width + HALO:
                begin = max(first, width + HALO)
                start = (turn + (parts - 1) * width + offset + begin - first) % LANES
                length = first + count - begin
                shift = start - at - (begin - width - HALO)
                value = jnp.where(within(start, length), roll(remote, shift), value)
        return value

    for group in range(-(-pieces // parts)):
        values = [
            piece_with_halo(group * parts + j) if group * parts + j < pieces else None for j in range(parts)
        ]
        for m in range(parts):
            turn = (slot - (me ^ m)) & (parts - 1)
            value = values[0]
            for j in range(1, parts):
                if values[j] is not None:
                    value = jnp.where(turn == j, values[j], value)
            outs[m][group] = value


class Geometry:
    def __init__(self, plan):
        self.plan = plan
        width, cols, parts = plan.width, plan.cols, plan.parts
        me, ty, ty_last = lax.axis_index("tx"), lax.axis_index("ty"), lax.axis_size("ty") - 1
        lane = lane_iota()
        self.offset_of = lane & (width - 1)
        slot = lane // width
        self.row_of, self.column_of = [], []
        for tile in range(plan.tiles):
            row = None
            for seg_tile, column, first, count, offset in plan.segments:
                if seg_tile == tile:
                    here_row, here_col = self.offset_of - offset + first, slot * cols + column
                    if row is None:
                        row, col = here_row, here_col
                    else:
                        inside = (self.offset_of >= offset) & (self.offset_of < offset + count)
                        row, col = jnp.where(inside, here_row, row), jnp.where(inside, here_col, col)
            self.row_of.append(row)
            self.column_of.append(col)
        block_row = me * width - HALO
        self.inner = {
            "west": [col > 0 for col in self.column_of],
            "east": [col < parts * cols - 1 for col in self.column_of],
            "south": [(row + block_row != 0) | (ty != 0) for row in self.row_of],
            "north": [(row + block_row != parts * width - 1) | (ty != ty_last) for row in self.row_of],
        }
        self.moves = {side: plan.moves(side) for side in self.inner}

    def neighbour(self, values, side):
        return shifted(values, self.moves[side], self.offset_of)

    def kept(self, side, tile, value):
        return jnp.where(self.inner[side][tile], value, 0.0)


SIDES = (
    ("west", "east", pl.ds(0, NP), -1.0),
    ("east", "west", pl.ds(NODES - NP, NP), 1.0),
    ("south", "north", pl.ds(0, NP, stride=NP), -1.0),
    ("north", "south", pl.ds(NP - 1, NP, stride=NP), 1.0),
)


def cut(value, i):
    return value[i * NP : (i + 1) * NP]


def section_adjoint(s, geometry, lift, adj_table, state, wet, speed, rub, final, later, total, gathered):
    half, drive = 0.5 * lift, PENALTY_SPEED
    neighbour, kept = geometry.neighbour, geometry.kept
    every = range(geometry.plan.tiles)
    comps = (0, 1, 2) if s < 3 else (1, 2)
    given = [WEIGHTS[s] * wet[s, t] for t in every]
    passed = [COEFS[s] * wet[s, t] if s < 3 else None for t in every]

    def masked(t, c, rows):
        value = given[t] * final[t, c - 1, rows] if c else None
        if s < 3:
            carried = passed[t] * later[s + 1, t, c, rows]
            value = carried if value is None else value + carried
        return value

    trace = {(name, c, t): masked(t, c, rows) for name, _, rows, _ in SIDES for c in comps for t in every}
    pulls, direct = {}, {}
    for name, other, _, sign in SIDES:
        for c in comps:
            beside = neighbour([trace[other, c, t] for t in every], name)
            for t in every:
                own = trace[name, c, t]
                pulls[name, c, t] = kept(name, t, (sign * half) * (own + beside[t]))
                direct[name, c, t] = kept(name, t, (half * drive) * (beside[t] - own))
    for t in every:
        cots = [[masked(t, c, pl.ds(i * NP, NP)) for i in range(NP)] for c in range(3)]
        ends = lambda c: [table[name, c, t] for table in (pulls, direct) for name in ("south", "north")]
        data = jnp.concatenate([split_data(cots[c], ends(c)) for c in comps], axis=1)
        out = jnp.dot(adj_table[...], data, preferred_element_type=F32)
        columns = {c: out[:, at * LANES : (at + 1) * LANES] for at, c in enumerate(comps)}
        for i in range(NP):
            rows = pl.ds(i * NP, NP)
            pull_x, pull_y, adds = (
                {c: cut(columns[c], k * NP + i) for c in comps} for k in range(3)
            )
            x_m, mixed, y_n = pull_x[1], pull_y[1] + pull_x[2], pull_y[2]
            to_m, to_n = adds[1], adds[2]
            if s < 3:
                to_m, to_n, to_h = to_m + pull_x[0], to_n + pull_y[0], adds[0]
            for at, name in ((0, "west"), (NP - 1, "east")):
                if i == at:
                    x_m = x_m + pulls[name, 1, t]
                    mixed = mixed + pulls[name, 2, t]
                    to_m = to_m + direct[name, 1, t]
                    to_n = to_n + direct[name, 2, t]
                    if s < 3:
                        to_m = to_m + pulls[name, 0, t]
                        to_h = to_h + direct[name, 0, t]
            h, u, v = state[s, t, 0, rows], speed[s, t, 0, rows], speed[s, t, 1, rows]
            cot_m, cot_n = cots[1][i], cots[2][i]
            drag, over = rub[s, t, 0, rows], rub[s, t, 1, rows]
            along = cot_m * u + cot_n * v
            fall = drag * along
            extra = over * along
            if gathered is not None:
                gathered[t] = gathered[t] + fall * h
            ux, vy = u * x_m, v * y_n
            first = ux + v * mixed + extra * u
            second = vy + extra * v
            later_h = h * (x_m + y_n) - u * first - v * second - (4.0 / 3.0) * fall
            if s < 3:
                later_h = later_h + to_h
            later_m = to_m + ux + first + drag * cot_m
            later_n = to_n + (vy + u * mixed) + second + drag * cot_n
            for c, value in enumerate((later_h, later_m, later_n)):
                if s == 0:
                    value = value + (later[1, t, c, rows] + later[2, t, c, rows] + later[3, t, c, rows])
                    if c:
                        value = value + final[t, c - 1, rows]
                    total[t, c, rows] = value
                else:
                    later[s, t, c, rows] = value


def step_kernel(plan, lift, *refs):
    parts, width, tiles = plan.parts, plan.width, plan.tiles
    messages = refs[:parts]
    man_ref, fwd_table, adj_table = refs[parts : parts + 3]
    rough_out, state, wet, speed, rub, final, later = refs[parts + 3 : parts + 10]
    weight, drop = refs[parts + 10 :]
    me = lax.axis_index("tx")
    zones = man_ref.shape[1]
    half, drive = 0.5 * lift, PENALTY_SPEED
    every = range(tiles)

    aux = [None] * tiles
    for n, value in exchange_in(
        lambda m, group: messages[m][group], len(SOURCES) * tiles, me, parts, width
    ):
        (array, i), tile = SOURCES[n // tiles], n % tiles
        if array < 3:
            state[0, tile, array, pl.ds(i * NP, NP)] = value
        elif array == 3:
            weight[tile, pl.ds(i * NP, NP)] = value
        else:
            aux[tile] = value
    geometry = Geometry(plan)
    neighbour, kept, row_of = geometry.neighbour, geometry.kept, geometry.row_of
    zone_iota = lax.broadcasted_iota(jnp.int32, (zones, LANES), 0).astype(F32)
    hot = []
    rough = []
    man = jnp.broadcast_to(man_ref[...], (8, zones))
    for tile in range(tiles):
        for s in range(4):
            wet[s, tile] = jnp.broadcast_to(aux[tile][s : s + 1], (8, LANES))
        hot.append((jnp.broadcast_to(aux[tile][4:5], (zones, LANES)) == zone_iota).astype(F32))
        rough.append(jnp.dot(man, hot[tile], precision=lax.Precision.HIGHEST, preferred_element_type=F32))
        drop[tile] = -(rough[tile] * rough[tile])

    for s in range(4):
        comps = (0, 1, 2) if s < 3 else (1, 2)
        for t in every:
            for i in range(NP):
                rows = pl.ds(i * NP, NP)
                h, m, n = (state[s, t, c, rows] for c in range(3))
                inverse = 1.0 / h
                u, v = m * inverse, n * inverse
                square = u * u + v * v + SPEED_FLOOR
                over = drop[t] * (lax.rsqrt(square) * jnp.exp((-4.0 / 3.0) * jnp.log(h)))
                speed[s, t, 0, rows] = u
                speed[s, t, 1, rows] = v
                rub[s, t, 0, rows] = over * square
                rub[s, t, 1, rows] = over
        hands, keeps = {}, {}
        for name, _, rows, sign in SIDES:
            for t in every:
                h, m, n = (state[s, t, c, rows] for c in range(3))
                pressure = 0.5 * h * h
                if name in ("west", "east"):
                    u = speed[s, t, 0, rows]
                    parts_of = (m, m * u + pressure, n * u)
                else:
                    v = speed[s, t, 1, rows]
                    parts_of = (n, m * v, n * v + pressure)
                for c in comps:
                    f, q = parts_of[c], (sign * drive) * (h, m, n)[c]
                    hands[name, c, t] = f + q
                    keeps[name, c, t] = f - q
        gains = {}
        for name, other, _, sign in SIDES:
            for c in comps:
                beside = neighbour([hands[other, c, t] for t in every], name)
                for t in every:
                    gains[name, c, t] = kept(name, t, (sign * half) * (keeps[name, c, t] - beside[t]))
        for t in every:
            fluxes = [[] for _ in range(5)]
            for i in range(NP):
                rows = pl.ds(i * NP, NP)
                h, m, n = (state[s, t, c, rows] for c in range(3))
                u, v = speed[s, t, 0, rows], speed[s, t, 1, rows]
                pressure = 0.5 * h * h
                for k, value in enumerate((m, n, m * u + pressure, n * u, n * v + pressure)):
                    fluxes[k].append(value)
            columns = []
            for c in comps:
                first, second = ((0, 1), (2, 3), (3, 4))[c]
                columns.append(
                    split_data(fluxes[first] + fluxes[second], [gains["south", c, t], gains["north", c, t]])
                )
            out = jnp.dot(
                fwd_table[...], jnp.concatenate(columns, axis=1), preferred_element_type=F32
            )
            now = (COEFS[s] if s < 3 else WEIGHTS[3]) * wet[s, t]
            for at, c in enumerate(comps):
                for i in range(NP):
                    rows = pl.ds(i * NP, NP)
                    value = cut(out[:, at * LANES : (at + 1) * LANES], i)
                    if i == 0:
                        value = value + gains["west", c, t]
                    if i == NP - 1:
                        value = value + gains["east", c, t]
                    if c:
                        value = value + rub[s, t, 0, rows] * state[s, t, c, rows]
                    start = state[0, t, c, rows]
                    if s < 3:
                        state[s + 1, t, c, rows] = start + now * value
                    else:
                        middle = state[1, t, c, rows] + 2.0 * state[2, t, c, rows] + state[3, t, c, rows]
                        total = ((1.0 / 3.0) * middle - (1.0 / 3.0) * start) + now * value
                        final[t, c - 1, rows] = weight[t, rows] * total

    gathered = [jnp.zeros((8, LANES), F32) for _ in every]
    for s in (3, 2, 1):
        section_adjoint(
            s, geometry, lift, adj_table, state, wet, speed, rub, final, later, None, gathered
        )
    gather_first(state, wet, speed, rub, final, later, gathered)

    part = jnp.zeros((8, zones), F32)
    for tile in range(tiles):
        own_rows = (row_of[tile] >= HALO) & (row_of[tile] < HALO + width)
        sums = jnp.broadcast_to(jnp.sum(gathered[tile], axis=0, keepdims=True), (8, LANES))
        sums = jnp.where(own_rows, 2.0 * sums / rough[tile], 0.0)
        part = part + lax.dot_general(
            sums,
            hot[tile],
            (((1,), (1,)), ((), ())),
            precision=lax.Precision.HIGHEST,
            preferred_element_type=F32,
        )
    rough_out[...] = jnp.concatenate([part, jnp.zeros((8, LANES - zones), F32)], axis=1)


def gather_first(state, wet, speed, rub, final, later, gathered):
    for t in range(len(gathered)):
        given, passed = WEIGHTS[0] * wet[0, t], COEFS[0] * wet[0, t]
        for i in range(NP):
            rows = pl.ds(i * NP, NP)
            cot_m, cot_n = (given * final[t, c - 1, rows] + passed * later[1, t, c, rows] for c in (1, 2))
            along = cot_m * speed[0, t, 0, rows] + cot_n * speed[0, t, 1, rows]
            gathered[t] = gathered[t] + rub[0, t, 0, rows] * along * state[0, t, 0, rows]


def answer_kernel(plan, lift, adj_table, state, wet, speed, rub, final, later, *refs):
    parts, width, cols = plan.parts, plan.width, plan.cols
    outs, total = refs[:parts], refs[parts]
    me = lax.axis_index("tx")
    geometry = Geometry(plan)
    offset_of = geometry.offset_of
    section_adjoint(0, geometry, lift, adj_table, state, wet, speed, rub, final, later, total, None)

    def own_piece(c, i, column):
        value = None
        for tile, seg_col, first, count, offset in plan.segments:
            begin, end = max(first, HALO), min(first + count, HALO + width)
            if seg_col != column or begin >= end:
                continue
            moved = roll(total[tile, c, pl.ds(i * NP, NP)], (begin - HALO) - (offset + begin - first))
            if value is None:
                value = moved
            else:
                value = jnp.where((offset_of >= begin - HALO) & (offset_of < end - HALO), moved, value)
        return value

    pieces = [
        functools.partial(own_piece, c, i, column) for c in range(3) for i in range(NP) for column in range(cols)
    ]

    def put(m, group, value):
        outs[m][group] = value

    exchange_out(pieces, put, me, parts, width)


def stamp_kernel(parts, *refs):
    mine, other, outs = refs[parts], refs[parts + 1], refs[parts + 2 :]
    total = mine[...] + other[...]
    for out in outs:
        out[out.shape[0] - 1] = total


def finish_kernel(plan, *refs):
    parts, width, cols = plan.parts, plan.width, plan.cols
    messages = refs[:parts]
    (out,) = refs[parts:]
    me = lax.axis_index("tx")
    count = 3 * NP * cols
    for n, value in exchange_in(lambda m, group: messages[m][group], count, me, parts, width):
        plane, column = n // cols, n % cols
        out[plane, pl.ds(column, NP, stride=cols), :] = value


def call(kernel, outs, scratch=(), flops=1000000):
    return pl.pallas_call(
        kernel,
        out_shape=outs,
        scratch_shapes=scratch,
        compiler_params=pltpu.CompilerParams(vmem_limit_bytes=16 << 20),
        cost_estimate=pl.CostEstimate(flops=flops, bytes_accessed=1000000, transcendentals=0),
    )


def xor_swap(value, axis, bits):
    count = lax.axis_size(axis)
    return lax.ppermute(value, axis, [(i, i ^ bits) for i in range(count)])


def sum_over(value, axis):
    count, bit = lax.axis_size(axis), 1
    while bit < count:
        if 4 * bit <= count:
            one, two, three = (xor_swap(value, axis, k * bit) for k in (1, 2, 3))
            value = (value + one) + (two + three)
            bit *= 4
        else:
            value = value + xor_swap(value, axis, bit)
            bit *= 2
    return value


def local(depth0, momentum0, obs_weight, wet_mask, zone_id, manning):
    table, lift = node_tables()
    cols, rows = depth0.shape[3], depth0.shape[4]
    parts = lax.axis_size("tx")
    plan = Plan(parts, cols, rows)
    zones = manning.shape[0]
    depth = depth0.reshape(NP, NP * cols, rows)
    momentum = momentum0.reshape(2 * NP, NP * cols, rows)
    weight = obs_weight.reshape(NP, NP * cols, rows)
    fields = (depth, momentum, weight, wet_mask, zone_id)

    def out(*shape):
        return jax.ShapeDtypeStruct(shape, F32)

    groups = -(-len(SOURCES) * cols // PER_VREG)
    inputs = fields + (manning.reshape(1, zones),)
    inputs = tuple(pltpu.with_memory_space_constraint(x, pltpu.HBM) for x in inputs)
    results = pl.pallas_call(
        functools.partial(halo_kernel, cols),
        out_shape=[jax.ShapeDtypeStruct(x.shape, x.dtype) for x in inputs] + [out(groups, 8, LANES)],
        in_specs=[pl.BlockSpec(memory_space=pltpu.HBM)] * 6,
        scratch_shapes=[pltpu.SemaphoreType.DMA((sum(len(chunks(x.shape[0])) for x in inputs),))],
        compiler_params=pltpu.CompilerParams(vmem_limit_bytes=16 << 20),
        cost_estimate=pl.CostEstimate(flops=1000000, bytes_accessed=1000000, transcendentals=0),
    )(*inputs)
    fields, man, halo = results[:5], results[5], results[6]
    if lax.axis_size("ty") > 1:
        assert lax.axis_size("ty") == 2
        halo = xor_swap(halo, "ty", 1)
    pieces = len(SOURCES) * plan.tiles
    count = -(-pieces // parts)
    turned = call(functools.partial(turn_kernel, plan), out(pieces, 8, LANES))(*fields)
    sent = call(functools.partial(pack_kernel, plan), [out(count, 8, LANES)] * parts)(turned, halo)
    received = [sent[0]] + [xor_swap(sent[m], "tx", m) for m in range(1, parts)]

    along_i, along_j = np.kron(table, np.eye(NP)), np.kron(np.eye(NP), table)
    ends = np.concatenate([np.kron(np.eye(NP), np.eye(NP)[:, k : k + 1]) for k in (0, NP - 1)], axis=1)
    none = np.zeros_like(ends)
    fwd_table = split_table(np.concatenate([-along_i, -along_j], axis=1), ends)
    adj_table = split_table(
        np.concatenate([-along_i.T, -along_j.T, np.zeros_like(along_i)], axis=0),
        np.block([[none, none], [ends, none], [none, ends]]),
    )
    back = -(-3 * NP * cols // parts)
    t = plan.tiles
    shapes = [
        (4, t, 3, NODES, LANES),
        (4, t, NP, LANES),
        (4, t, 2, NODES, LANES),
        (4, t, 2, NODES, LANES),
        (t, 2, NODES, LANES),
        (4, t, 3, NODES, LANES),
    ]
    tables = jnp.asarray(fwd_table), jnp.asarray(adj_table)
    rough, *kept = call(
        functools.partial(step_kernel, plan, lift),
        [out(8, LANES)] + [out(*shape) for shape in shapes],
        [pltpu.VMEM((t, NODES, LANES), F32), pltpu.VMEM((t, NP, LANES), F32)],
    )(*received, man, *tables)
    answers = call(
        functools.partial(answer_kernel, plan, lift),
        [out(back + 1, 8, LANES)] * parts,
        [pltpu.VMEM((t, 3, NODES, LANES), F32)],
    )(tables[1], *kept)
    other = jnp.zeros_like(rough)
    if lax.axis_size("ev") == 2:
        other = xor_swap(rough, "ev", 1)
    elif lax.axis_size("ev") > 1:
        rough = sum_over(rough, "ev")
    space = pl.BlockSpec(memory_space=pltpu.VMEM)
    answers = pl.pallas_call(
        functools.partial(stamp_kernel, parts),
        out_shape=[out(back + 1, 8, LANES)] * parts,
        in_specs=[pl.BlockSpec(memory_space=pl.ANY)] * parts + [space] * 2,
        out_specs=[space] * parts,
        input_output_aliases={m: m for m in range(parts)},
        compiler_params=pltpu.CompilerParams(vmem_limit_bytes=16 << 20),
        cost_estimate=pl.CostEstimate(flops=1000, bytes_accessed=1000, transcendentals=0),
    )(*answers, rough, other)
    answers = [answers[0]] + [xor_swap(answers[m], "tx", m) for m in range(1, parts)]
    sums = [answer[back] for answer in answers]
    while len(sums) > 1:
        sums = [one + two for one, two in zip(sums[::2], sums[1::2])]
    rough = sum_over(sums[0], "ty")
    adjoint = call(functools.partial(finish_kernel, plan), out(3 * NP, NP * cols, rows))(*answers)
    events_all = depth0.shape[0] * lax.axis_size("ev")
    scale = zones / (TIME_STEP * events_all * cols * parts * rows * lax.axis_size("ty") * NODES)
    return (adjoint.reshape(1, 3, NP, NP, cols, rows), rough[0, :zones] * scale)


def solution(mesh):
    in_specs = (
        P(("basin", "ev"), None, None, "tx", "ty"),
        P(("basin", "ev"), None, None, None, "tx", "ty"),
        P(("basin", "ev"), None, None, "tx", "ty"),
        P(("basin", "ev"), None, "tx", "ty"),
        P(("basin", "tx"), "ty"),
        P("basin"),
    )
    out_specs = (P(("basin", "ev"), None, None, None, "tx", "ty"), P("basin"))
    return jax.shard_map(local, mesh=mesh, in_specs=in_specs, out_specs=out_specs, check_vma=False)
```

profile of v0, /device:TPU:0, one launch (start us, length us, event | category | flops | bytes accessed | tf_op | source)
XLA Modules:
  0.0 35.1 jit_solution(4460046077101715703)
XLA Ops:
  0.6 0.0 copy-start
  0.6 0.0 copy-start.1
  0.7 1.2 %shard_map.95 = (f32[8,16,128]{2,1,0:T(8,128)S(1)}, f32[16,16,128]{2,1,0:T(8,128)S(1)}, f32[8,16,128]{2,1,0:T(8,128)S(1)}, s32[1,4,2,128]{3,2,1,0:T(2,128)S(1)},...) custom-call(f32[8,16,128]{2,1,0:T(8,128)} %bitcast.11, f32[16,16,128]{2,1,0:T(8,128)} %bitcast.10, ...), custom_call_target="tpu_custom_call" | custom-call | flops 1000000 | bytes 1000000 | tf_op jit(solution)/shard_map/pallas_call | solution.py:643
  1.8 0.6 %collective-permute-start = (f32[5,8,128]{2,1,0:T(8,128)S(1)}, f32[5,8,128]{2,1,0:T(8,128)S(1)}, u32[]{:S(2)}, u32[]{:S(2)}) collective-permute-start(f32[5,8,128]{2,1,0:T(8,128)S(1)} %get-tuple-element.33), channel_id=1, source_target_pairs={{0,2},{2,0},{1,3},{3,1},{4,6},{6,4},{5,7},{7,5},{8,10},{10,8},{9,1... | collective-permute-start | bytes 61448 | tf_op jit(solution)/shard_map/ppermute | solution.py:610
  2.4 0.2 shard_map.96.turned
  2.6 0.6 %collective-permute-done.halo = f32[5,8,128]{2,1,0:T(8,128)S(1)} collective-permute-done((f32[5,8,128]{2,1,0:T(8,128)S(1)}, f32[5,8,128]{2,1,0:T(8,128)S(1)}, u32[]{:S(2)}, u32[]{:S(2)}) %collective-permute-start) | collective-permute-done | bytes 20512 | tf_op jit(solution)/shard_map/ppermute | solution.py:610
  3.2 0.2 shard_map.97
  3.4 3.0 %collective-permute-start.1 = (f32[25,8,128]{2,1,0:T(8,128)S(1)}, f32[25,8,128]{2,1,0:T(8,128)S(1)}, u32[]{:S(2)}, u32[]{:S(2)}) collective-permute-start(f32[25,8,128]{2,1,0:T(8,128)S(1)} %get-tuple-element.35), channel_id=1, source_target_pairs={{0,4},{4,0},{8,12},{12,8},{1,5},{5,1},{9,13},{13,9},{2,6},{6,2},{1... | collective-permute-start | bytes 307208 | tf_op jit(solution)/shard_map/ppermute | solution.py:610
  6.4 2.6 %collective-permute-start.2 = (f32[25,8,128]{2,1,0:T(8,128)S(1)}, f32[25,8,128]{2,1,0:T(8,128)S(1)}, u32[]{:S(2)}, u32[]{:S(2)}) collective-permute-start(f32[25,8,128]{2,1,0:T(8,128)S(1)} %get-tuple-element.36), channel_id=1, source_target_pairs={{0,8},{4,12},{8,0},{12,4},{1,9},{5,13},{9,1},{13,5},{2,10},{6,14},... | collective-permute-start | bytes 307208 | tf_op jit(solution)/shard_map/ppermute | solution.py:610
  9.0 0.0 collective-permute-start.3
  9.0 0.6 %collective-permute-done.1.refs_1_ = f32[25,8,128]{2,1,0:T(8,128)S(1)} collective-permute-done((f32[25,8,128]{2,1,0:T(8,128)S(1)}, f32[25,8,128]{2,1,0:T(8,128)S(1)}, u32[]{:S(2)}, u32[]{:S(2)}) %collective-permute-start.1) | collective-permute-done | bytes 102432 | tf_op jit(solution)/shard_map/ppermute | solution.py:610
  9.6 7.7 %collective-permute-done.2.refs_2_ = f32[25,8,128]{2,1,0:T(8,128)S(1)} collective-permute-done((f32[25,8,128]{2,1,0:T(8,128)S(1)}, f32[25,8,128]{2,1,0:T(8,128)S(1)}, u32[]{:S(2)}, u32[]{:S(2)}) %collective-permute-start.2) | collective-permute-done | bytes 102432 | tf_op jit(solution)/shard_map/ppermute | solution.py:610
  17.3 0.0 collective-permute-done.3.refs_3_
  17.3 0.0 copy-done
  17.3 0.0 copy-done.1
  17.3 3.3 %shard_map.98 = (f32[8,128]{1,0:T(8,128)S(1)}, f32[4,3,3,64,128]{4,3,2,1,0:T(8,128)S(1)}, f32[4,3,8,128]{3,2,1,0:T(8,128)S(1)}, f32[4,3,2,64,128]{4,3,2,1,0:T(8,...) custom-call(f32[25,8,128]{2,1,0:T(8,128)S(1)} %get-tuple-element.34.re, ...), custom_call_target="tpu_custom_call" | custom-call | flops 1000000 | bytes 1000000 | tf_op jit(solution)/shard_map/pallas_call | solution.py:680
  20.6 1.5 %collective-permute-start.4 = (f32[8,128]{1,0:T(8,128)S(1)}, f32[8,128]{1,0:T(8,128)S(1)}, u32[]{:S(2)}, u32[]{:S(2)}) collective-permute-start(f32[8,128]{1,0:T(8,128)S(1)} %get-tuple-element.49.refs_4_), channel_id=1, source_target_pairs={{0,1},{1,0},{2,3},{3,2},{4,5},{5,4},{6,7},{7,6},{8,9},{9,8},{10,11... | collective-permute-start | bytes 12296 | tf_op jit(solution)/shard_map/ppermute | solution.py:610
  22.1 0.7 %shard_map.99 = (f32[13,8,128]{2,1,0:T(8,128)S(1)}, f32[13,8,128]{2,1,0:T(8,128)S(1)}, f32[13,8,128]{2,1,0:T(8,128)S(1)}, f32[13,8,128]{2,1,0:T(8,128)S(1)}) custom-call(bf16[192,256]{1,0:T(8,128)(2,1)S(1)} %copy-done, f32[4,3,3,64,128]{4,3,2,1,0:T(8,128)S(1)} %get-tuple-element.39.state, f32[4,3,8,128]{3,2,1,0:T(8,128)S(1)} %get-tuple-element.40.wet, ...), custom_call_target="tpu_custom_call" | custom-call | flops 1000000 | bytes 1000000 | tf_op jit(solution)/shard_map/pallas_call | solution.py:685
  22.8 1.5 %collective-permute-done.4.refs_5_ = f32[8,128]{1,0:T(8,128)S(1)} collective-permute-done((f32[8,128]{1,0:T(8,128)S(1)}, f32[8,128]{1,0:T(8,128)S(1)}, u32[]{:S(2)}, u32[]{:S(2)}) %collective-permute-start.4) | collective-permute-done | bytes 4128 | tf_op jit(solution)/shard_map/ppermute | solution.py:610
  24.3 1.8 %collective-permute-start.5 = (f32[13,8,128]{2,1,0:T(8,128)S(1)}, f32[13,8,128]{2,1,0:T(8,128)S(1)}, u32[]{:S(2)}, u32[]{:S(2)}) collective-permute-start(f32[13,8,128]{2,1,0:T(8,128)S(1)} %get-tuple-element.51), channel_id=1, source_target_pairs={{0,4},{4,0},{8,12},{12,8},{1,5},{5,1},{9,13},{13,9},{2,6},{6,2},{1... | collective-permute-start | bytes 159752 | tf_op jit(solution)/shard_map/ppermute | solution.py:610
  26.1 1.4 %collective-permute-start.6 = (f32[13,8,128]{2,1,0:T(8,128)S(1)}, f32[13,8,128]{2,1,0:T(8,128)S(1)}, u32[]{:S(2)}, u32[]{:S(2)}) collective-permute-start(f32[13,8,128]{2,1,0:T(8,128)S(1)} %get-tuple-element.52), channel_id=1, source_target_pairs={{0,8},{4,12},{8,0},{12,4},{1,9},{5,13},{9,1},{13,5},{2,10},{6,14},... | collective-permute-start | bytes 159752 | tf_op jit(solution)/shard_map/ppermute | solution.py:610
  27.4 1.2 %collective-permute-start.7 = (f32[13,8,128]{2,1,0:T(8,128)S(1)}, f32[13,8,128]{2,1,0:T(8,128)S(1)}, u32[]{:S(2)}, u32[]{:S(2)}) collective-permute-start(f32[13,8,128]{2,1,0:T(8,128)S(1)} %get-tuple-element.53), channel_id=1, source_target_pairs={{0,12},{4,8},{8,4},{12,0},{1,13},{5,9},{9,5},{13,1},{2,14},{6,10},... | collective-permute-start | bytes 159752 | tf_op jit(solution)/shard_map/ppermute | solution.py:610
  28.7 0.0 collective-permute-done.5.refs_1_
  28.7 3.0 %collective-permute-done.6.refs_2_ = f32[13,8,128]{2,1,0:T(8,128)S(1)} collective-permute-done((f32[13,8,128]{2,1,0:T(8,128)S(1)}, f32[13,8,128]{2,1,0:T(8,128)S(1)}, u32[]{:S(2)}, u32[]{:S(2)}) %collective-permute-start.6) | collective-permute-done | bytes 53280 | tf_op jit(solution)/shard_map/ppermute | solution.py:610
  31.7 1.7 %collective-permute-done.7.refs_3_ = f32[13,8,128]{2,1,0:T(8,128)S(1)} collective-permute-done((f32[13,8,128]{2,1,0:T(8,128)S(1)}, f32[13,8,128]{2,1,0:T(8,128)S(1)}, u32[]{:S(2)}, u32[]{:S(2)}) %collective-permute-start.7) | collective-permute-done | bytes 53280 | tf_op jit(solution)/shard_map/ppermute | solution.py:610
  33.4 0.0 collective-permute-start.8
  33.4 0.9 %shard_map.101 = f32[24,16,128]{2,1,0:T(8,128)} custom-call(f32[13,8,128]{2,1,0:T(8,128)S(1)} %get-tuple-element.50.refs_0_, f32[13,8,128]{2,1,0:T(8,128)S(1)} %collective-permute-done.5.refs_1_, f32[13,8,128]{2,1,0:T(8,128)S(1)} %collective-permute-done.6.refs_2_, f32[13,8,128]{2,1,0:T(8,128)S(1)} %collective-permute-done.7.refs_3_), custom_call_target="tpu_custom_call" | custom-call | flops 1000000 | bytes 1000000 | tf_op jit(solution)/shard_map/pallas_call | solution.py:710
  34.3 0.3 collective-permute-done.8
  34.6 0.5 %multiply_bitcast_fusion = f32[32]{0:T(128)} fusion(f32[8,128]{1,0:T(8,128)S(1)} %add.21), kind=kLoop, calls=%fused_computation.4 | loop fusion | flops 32 | bytes 256 | tf_op jit(solution)/shard_map/mul | solution.py:713
  (3 shorter events, 0.0 us)
Async XLA Ops:
  0.6 16.7 %copy-start = (bf16[192,256]{1,0:T(8,128)(2,1)S(1)}, bf16[192,256]{1,0:T(8,128)(2,1)}, u32[]{:S(2)}) copy-start(bf16[192,256]{1,0:T(8,128)(2,1)} %constant.7.clone.refs_6_.adj_table) | copy-start | bytes 294916
  0.6 16.7 %copy-start.1 = (bf16[64,416]{1,0:T(8,128)(2,1)S(1)}, bf16[64,416]{1,0:T(8,128)(2,1)}, u32[]{:S(2)}) copy-start(bf16[64,416]{1,0:T(8,128)(2,1)} %constant.6.clone.refs_5_) | copy-start | bytes 159748
  1.8 1.4 %collective-permute-start = (f32[5,8,128]{2,1,0:T(8,128)S(1)}, f32[5,8,128]{2,1,0:T(8,128)S(1)}, u32[]{:S(2)}, u32[]{:S(2)}) collective-permute-start(f32[5,8,128]{2,1,0:T(8,128)S(1)} %get-tuple-element.33), channel_id=1, source_target_pairs={{0,2},{2,0},{1,3},{3,1},{4,6},{6,4},{5,7},{7,5},{8,10},{10,8},{9,1... | collective-permute-start | bytes 61448 | tf_op jit(solution)/shard_map/ppermute | solution.py:610
  3.4 6.2 %collective-permute-start.1 = (f32[25,8,128]{2,1,0:T(8,128)S(1)}, f32[25,8,128]{2,1,0:T(8,128)S(1)}, u32[]{:S(2)}, u32[]{:S(2)}) collective-permute-start(f32[25,8,128]{2,1,0:T(8,128)S(1)} %get-tuple-element.35), channel_id=1, source_target_pairs={{0,4},{4,0},{8,12},{12,8},{1,5},{5,1},{9,13},{13,9},{2,6},{6,2},{1... | collective-permute-start | bytes 307208 | tf_op jit(solution)/shard_map/ppermute | solution.py:610
  6.4 10.9 %collective-permute-start.2 = (f32[25,8,128]{2,1,0:T(8,128)S(1)}, f32[25,8,128]{2,1,0:T(8,128)S(1)}, u32[]{:S(2)}, u32[]{:S(2)}) collective-permute-start(f32[25,8,128]{2,1,0:T(8,128)S(1)} %get-tuple-element.36), channel_id=1, source_target_pairs={{0,8},{4,12},{8,0},{12,4},{1,9},{5,13},{9,1},{13,5},{2,10},{6,14},... | collective-permute-start | bytes 307208 | tf_op jit(solution)/shard_map/ppermute | solution.py:610
  9.0 8.3 %collective-permute-start.3 = (f32[25,8,128]{2,1,0:T(8,128)S(1)}, f32[25,8,128]{2,1,0:T(8,128)S(1)}, u32[]{:S(2)}, u32[]{:S(2)}) collective-permute-start(f32[25,8,128]{2,1,0:T(8,128)S(1)} %get-tuple-element.37), channel_id=1, source_target_pairs={{0,12},{4,8},{8,4},{12,0},{1,13},{5,9},{9,5},{13,1},{2,14},{6,10},... | collective-permute-start | bytes 307208 | tf_op jit(solution)/shard_map/ppermute | solution.py:610
  20.6 3.6 %collective-permute-start.4 = (f32[8,128]{1,0:T(8,128)S(1)}, f32[8,128]{1,0:T(8,128)S(1)}, u32[]{:S(2)}, u32[]{:S(2)}) collective-permute-start(f32[8,128]{1,0:T(8,128)S(1)} %get-tuple-element.49.refs_4_), channel_id=1, source_target_pairs={{0,1},{1,0},{2,3},{3,2},{4,5},{5,4},{6,7},{7,6},{8,9},{9,8},{10,11... | collective-permute-start | bytes 12296 | tf_op jit(solution)/shard_map/ppermute | solution.py:610
  24.3 4.4 %collective-permute-start.5 = (f32[13,8,128]{2,1,0:T(8,128)S(1)}, f32[13,8,128]{2,1,0:T(8,128)S(1)}, u32[]{:S(2)}, u32[]{:S(2)}) collective-permute-start(f32[13,8,128]{2,1,0:T(8,128)S(1)} %get-tuple-element.51), channel_id=1, source_target_pairs={{0,4},{4,0},{8,12},{12,8},{1,5},{5,1},{9,13},{13,9},{2,6},{6,2},{1... | collective-permute-start | bytes 159752 | tf_op jit(solution)/shard_map/ppermute | solution.py:610
  26.1 5.6 %collective-permute-start.6 = (f32[13,8,128]{2,1,0:T(8,128)S(1)}, f32[13,8,128]{2,1,0:T(8,128)S(1)}, u32[]{:S(2)}, u32[]{:S(2)}) collective-permute-start(f32[13,8,128]{2,1,0:T(8,128)S(1)} %get-tuple-element.52), channel_id=1, source_target_pairs={{0,8},{4,12},{8,0},{12,4},{1,9},{5,13},{9,1},{13,5},{2,10},{6,14},... | collective-permute-start | bytes 159752 | tf_op jit(solution)/shard_map/ppermute | solution.py:610
  27.4 5.9 %collective-permute-start.7 = (f32[13,8,128]{2,1,0:T(8,128)S(1)}, f32[13,8,128]{2,1,0:T(8,128)S(1)}, u32[]{:S(2)}, u32[]{:S(2)}) collective-permute-start(f32[13,8,128]{2,1,0:T(8,128)S(1)} %get-tuple-element.53), channel_id=1, source_target_pairs={{0,12},{4,8},{8,4},{12,0},{1,13},{5,9},{9,5},{13,1},{2,14},{6,10},... | collective-permute-start | bytes 159752 | tf_op jit(solution)/shard_map/ppermute | solution.py:610
  33.4 1.2 %collective-permute-start.8 = (f32[8,128]{1,0:T(8,128)S(1)}, f32[8,128]{1,0:T(8,128)S(1)}, u32[]{:S(2)}, u32[]{:S(2)}) collective-permute-start(f32[8,128]{1,0:T(8,128)S(1)} %fusion.1), channel_id=1, source_target_pairs={{0,2},{2,0},{1,3},{3,1},{4,6},{6,4},{5,7},{7,5},{8,10},{10,8},{9,1... | collective-permute-start | bytes 12296 | tf_op jit(solution)/shard_map/ppermute | solution.py:610
where the time goes:
time: 35.2 us; the launch traced here: 35.1 us
  waiting for transfers between devices  15.4 us (44%)
  starting transfers between devices  12 us (34%)
  Pallas kernels  6.42 us (18%)
  between operations  0.68 us (2%)
  other arithmetic  0.52 us (1%)
    ppermute x9, waiting for transfers between devices, xor_swap(): return lax.ppermute(value, axis, [(i, i ^ bits) for i in range(count)])  15.4 us
    ppermute x9, starting transfers between devices, xor_swap(): return lax.ppermute(value, axis, [(i, i ^ bits) for i in range(count)])  12 us
    pallas_call x1, Pallas kernels, local(): call(functools.partial(step_kernel, plan, lift), [out(8, LANES)] + [out(*...  3.32 us
    pallas_call x1, Pallas kernels, local(): pl.pallas_call(functools.partial(halo_kernel, cols), out_shape=[jax.Shape...  1.16 us
    pallas_call x1, Pallas kernels, local(): call(functools.partial(finish_kernel, plan), out(3 * NP, NP * cols, rows))  0.89 us
  transfers between devices with their start and end apart: 9, of which 7 were waited for; matrix products, arithmetic and copies ran while one was open for 0% of the time, Pallas kernels for 5%

commit v1 on v0

--- a/solution.py
+++ b/solution.py
@@ -185,24 +185,29 @@
     return ref[index, pl.ds(column, NP, stride=cols), :]
 
 
-SOURCES = [(array, i) for array in range(4) for i in range(NP)] + [(4, 0)]
+EARLY = [(array, i) for array in range(3) for i in range(NP)] + [(4, 0)]
+LATE = [(3, i) for i in range(NP)]
+SOURCES = EARLY + LATE
 PER_VREG = LANES // HALO
 
 
 def chunks(count):
     size = NP // 2
-    return [pl.ds(k, size) for k in range(0, count, size)] if count % size == 0 else [pl.ds(0, count)]
+    whole = count % size != 0 or count > 2 * NP
+    return [pl.ds(0, count)] if whole else [pl.ds(k, size) for k in range(0, count, size)]
 
 
 def halo_kernel(cols, *refs):
-    sources, (copies, out, sems) = refs[:6], (refs[6:12], refs[12], refs[13])
+    count = (len(refs) - 2) // 2
+    sources, copies, out, sems = refs[:count], refs[count:-2], refs[-2], refs[-1]
     moves = []
     for src, dst in zip(sources, copies):
         for rows in chunks(src.shape[0]):
             moves.append(pltpu.make_async_copy(src.at[rows], dst.at[rows], sems.at[len(moves)]))
+    needed = sum(len(chunks(src.shape[0])) for src in sources[:5])
     for move in moves:
         move.start()
-    for move in moves:
+    for move in moves[:needed]:
         move.wait()
     first = lax.axis_index("ty") == 0
     base = jnp.where(first, HALO, 0)
@@ -219,46 +224,48 @@
                 )
                 value = jnp.where(slot == k, moved, value)
         out[group] = value
-
-
-def turn_kernel(plan, depth, momentum, weight, wet, zone, out):
+    for move in moves[needed:]:
+        move.wait()
+
+
+def turn_kernel(plan, depth, momentum, weight, wet, zone, *outs):
     refs = (depth, momentum, weight, wet, zone)
     offset_of = lane_iota() & (plan.width - 1)
-    for number, (array, i) in enumerate(SOURCES):
-        columns = [source_vreg(refs, array, i, column, plan.cols) for column in range(plan.cols)]
-        for tile in range(plan.tiles):
-            piece = number * plan.tiles + tile
-            turn = plan.width * (piece % plan.parts)
-            value = None
-            for seg_tile, column, first, count, offset in plan.segments:
-                if seg_tile == tile:
-                    own = roll(columns[column], turn + offset - (first - HALO))
-                    if value is None:
-                        value = own
-                    else:
-                        at = (offset_of >= offset) & (offset_of < offset + count)
-                        value = jnp.where(at, own, value)
-            out[piece] = value
-
-
-def pack_kernel(plan, turned, halo, *outs):
+    for sources, out in zip((EARLY, LATE), outs):
+        for number, (array, i) in enumerate(sources):
+            columns = [source_vreg(refs, array, i, column, plan.cols) for column in range(plan.cols)]
+            for tile in range(plan.tiles):
+                piece = number * plan.tiles + tile
+                turn = plan.width * (piece % plan.parts)
+                value = None
+                for seg_tile, column, first, count, offset in plan.segments:
+                    if seg_tile == tile:
+                        own = roll(columns[column], turn + offset - (first - HALO))
+                        if value is None:
+                            value = own
+                        else:
+                            at = (offset_of >= offset) & (offset_of < offset + count)
+                            value = jnp.where(at, own, value)
+                out[piece] = value
+
+
+def pack_kernel(plan, early, late, halo, *outs):
     me = lax.axis_index("tx")
     lane = lane_iota()
     cols, width, parts = plan.cols, plan.width, plan.parts
     slot = lane // width
-    pieces = turned.shape[0]
 
     def within(start, length):
         return ((lane - start) & (LANES - 1)) < length
 
-    def piece_with_halo(piece):
+    def piece_with_halo(turned, before, piece):
         number, tile = piece // plan.tiles, piece % plan.tiles
         turn = width * (piece % parts)
         value = turned[piece]
         for seg_tile, column, first, count, offset in plan.segments:
             if seg_tile != tile:
                 continue
-            n = number * cols + column
+            n = (before + number) * cols + column
             remote, at = halo[n // PER_VREG], HALO * (n % PER_VREG)
             if first < HALO:
                 start = (turn + offset) % LANES
@@ -271,17 +278,20 @@
                 value = jnp.where(within(start, length), roll(remote, shift), value)
         return value
 
-    for group in range(-(-pieces // parts)):
-        values = [
-            piece_with_halo(group * parts + j) if group * parts + j < pieces else None for j in range(parts)
-        ]
-        for m in range(parts):
-            turn = (slot - (me ^ m)) & (parts - 1)
-            value = values[0]
-            for j in range(1, parts):
-                if values[j] is not None:
-                    value = jnp.where(turn == j, values[j], value)
-            outs[m][group] = value
+    for turned, before, targets in ((early, 0, outs[:parts]), (late, len(EARLY), outs[parts:])):
+        pieces = turned.shape[0]
+        for group in range(-(-pieces // parts)):
+            values = [
+                piece_with_halo(turned, before, group * parts + j) if group * parts + j < pieces else None
+                for j in range(parts)
+            ]
+            for m in range(parts):
+                turn = (slot - (me ^ m)) & (parts - 1)
+                value = values[0]
+                for j in range(1, parts):
+                    if values[j] is not None:
+                        value = jnp.where(turn == j, values[j], value)
+                targets[m][group] = value
 
 
 class Geometry:
@@ -407,40 +417,37 @@
                     later[s, t, c, rows] = value
 
 
-def step_kernel(plan, lift, *refs):
+def roughness(man_ref, zone_row):
+    zones = man_ref.shape[1]
+    zone_iota = lax.broadcasted_iota(jnp.int32, (zones, LANES), 0).astype(F32)
+    hot = (jnp.broadcast_to(zone_row, (zones, LANES)) == zone_iota).astype(F32)
+    man = jnp.broadcast_to(man_ref[...], (8, zones))
+    return hot, jnp.dot(man, hot, precision=lax.Precision.HIGHEST, preferred_element_type=F32)
+
+
+def forward_kernel(plan, lift, *refs):
     parts, width, tiles = plan.parts, plan.width, plan.tiles
     messages = refs[:parts]
-    man_ref, fwd_table, adj_table = refs[parts : parts + 3]
-    rough_out, state, wet, speed, rub, final, later = refs[parts + 3 : parts + 10]
-    weight, drop = refs[parts + 10 :]
+    man_ref, fwd_table = refs[parts : parts + 2]
+    state, wet, speed, rub, final, zone, drop = refs[parts + 2 :]
     me = lax.axis_index("tx")
-    zones = man_ref.shape[1]
     half, drive = 0.5 * lift, PENALTY_SPEED
     every = range(tiles)
 
-    aux = [None] * tiles
     for n, value in exchange_in(
-        lambda m, group: messages[m][group], len(SOURCES) * tiles, me, parts, width
+        lambda m, group: messages[m][group], len(EARLY) * tiles, me, parts, width
     ):
-        (array, i), tile = SOURCES[n // tiles], n % tiles
+        (array, i), tile = EARLY[n // tiles], n % tiles
         if array < 3:
             state[0, tile, array, pl.ds(i * NP, NP)] = value
-        elif array == 3:
-            weight[tile, pl.ds(i * NP, NP)] = value
         else:
-            aux[tile] = value
+            for s in range(4):
+                wet[s, tile] = jnp.broadcast_to(value[s : s + 1], (8, LANES))
+            zone[tile] = value
+            rough = roughness(man_ref, value[4:5])[1]
+            drop[tile] = -(rough * rough)
     geometry = Geometry(plan)
-    neighbour, kept, row_of = geometry.neighbour, geometry.kept, geometry.row_of
-    zone_iota = lax.broadcasted_iota(jnp.int32, (zones, LANES), 0).astype(F32)
-    hot = []
-    rough = []
-    man = jnp.broadcast_to(man_ref[...], (8, zones))
-    for tile in range(tiles):
-        for s in range(4):
-            wet[s, tile] = jnp.broadcast_to(aux[tile][s : s + 1], (8, LANES))
-        hot.append((jnp.broadcast_to(aux[tile][4:5], (zones, LANES)) == zone_iota).astype(F32))
-        rough.append(jnp.dot(man, hot[tile], precision=lax.Precision.HIGHEST, preferred_element_type=F32))
-        drop[tile] = -(rough[tile] * rough[tile])
+    neighbour, kept = geometry.neighbour, geometry.kept
 
     for s in range(4):
         comps = (0, 1, 2) if s < 3 else (1, 2)
@@ -512,8 +519,27 @@
                     else:
                         middle = state[1, t, c, rows] + 2.0 * state[2, t, c, rows] + state[3, t, c, rows]
                         total = ((1.0 / 3.0) * middle - (1.0 / 3.0) * start) + now * value
-                        final[t, c - 1, rows] = weight[t, rows] * total
-
+                        final[t, c - 1, rows] = total
+
+
+def adjoint_kernel(plan, lift, *refs):
+    parts, width, tiles = plan.parts, plan.width, plan.tiles
+    messages = refs[:parts]
+    man_ref, adj_table, state, wet, speed, rub, reached, zone = refs[parts : parts + 8]
+    rough_out, final, later = refs[parts + 8 :]
+    me = lax.axis_index("tx")
+    zones = man_ref.shape[1]
+    every = range(tiles)
+    for n, value in exchange_in(
+        lambda m, group: messages[m][group], len(LATE) * tiles, me, parts, width
+    ):
+        i, tile = LATE[n // tiles][1], n % tiles
+        rows = pl.ds(i * NP, NP)
+        for c in range(2):
+            final[tile, c, rows] = value * reached[tile, c, rows]
+    geometry = Geometry(plan)
+    row_of = geometry.row_of
+    hot, rough = zip(*(roughness(man_ref, zone[t, 4:5]) for t in every))
     gathered = [jnp.zeros((8, LANES), F32) for _ in every]
     for s in (3, 2, 1):
         section_adjoint(
@@ -637,27 +663,6 @@
     def out(*shape):
         return jax.ShapeDtypeStruct(shape, F32)
 
-    groups = -(-len(SOURCES) * cols // PER_VREG)
-    inputs = fields + (manning.reshape(1, zones),)
-    inputs = tuple(pltpu.with_memory_space_constraint(x, pltpu.HBM) for x in inputs)
-    results = pl.pallas_call(
-        functools.partial(halo_kernel, cols),
-        out_shape=[jax.ShapeDtypeStruct(x.shape, x.dtype) for x in inputs] + [out(groups, 8, LANES)],
-        in_specs=[pl.BlockSpec(memory_space=pltpu.HBM)] * 6,
-        scratch_shapes=[pltpu.SemaphoreType.DMA((sum(len(chunks(x.shape[0])) for x in inputs),))],
-        compiler_params=pltpu.CompilerParams(vmem_limit_bytes=16 << 20),
-        cost_estimate=pl.CostEstimate(flops=1000000, bytes_accessed=1000000, transcendentals=0),
-    )(*inputs)
-    fields, man, halo = results[:5], results[5], results[6]
-    if lax.axis_size("ty") > 1:
-        assert lax.axis_size("ty") == 2
-        halo = xor_swap(halo, "ty", 1)
-    pieces = len(SOURCES) * plan.tiles
-    count = -(-pieces // parts)
-    turned = call(functools.partial(turn_kernel, plan), out(pieces, 8, LANES))(*fields)
-    sent = call(functools.partial(pack_kernel, plan), [out(count, 8, LANES)] * parts)(turned, halo)
-    received = [sent[0]] + [xor_swap(sent[m], "tx", m) for m in range(1, parts)]
-
     along_i, along_j = np.kron(table, np.eye(NP)), np.kron(np.eye(NP), table)
     ends = np.concatenate([np.kron(np.eye(NP), np.eye(NP)[:, k : k + 1]) for k in (0, NP - 1)], axis=1)
     none = np.zeros_like(ends)
@@ -666,6 +671,30 @@
         np.concatenate([-along_i.T, -along_j.T, np.zeros_like(along_i)], axis=0),
         np.block([[none, none], [ends, none], [none, ends]]),
     )
+    groups = -(-len(SOURCES) * cols // PER_VREG)
+    inputs = fields + (manning.reshape(1, zones), jnp.asarray(fwd_table), jnp.asarray(adj_table))
+    inputs = tuple(pltpu.with_memory_space_constraint(x, pltpu.HBM) for x in inputs)
+    results = pl.pallas_call(
+        functools.partial(halo_kernel, cols),
+        out_shape=[jax.ShapeDtypeStruct(x.shape, x.dtype) for x in inputs] + [out(groups, 8, LANES)],
+        in_specs=[pl.BlockSpec(memory_space=pltpu.HBM)] * len(inputs),
+        scratch_shapes=[pltpu.SemaphoreType.DMA((sum(len(chunks(x.shape[0])) for x in inputs),))],
+        compiler_params=pltpu.CompilerParams(vmem_limit_bytes=16 << 20),
+        cost_estimate=pl.CostEstimate(flops=1000000, bytes_accessed=1000000, transcendentals=0),
+    )(*inputs)
+    fields, man, tables, halo = results[:5], results[5], results[6:8], results[8]
+    if lax.axis_size("ty") > 1:
+        assert lax.axis_size("ty") == 2
+        halo = xor_swap(halo, "ty", 1)
+    pieces = [len(sources) * plan.tiles for sources in (EARLY, LATE)]
+    counts = [-(-count // parts) for count in pieces]
+    turned = call(functools.partial(turn_kernel, plan), [out(count, 8, LANES) for count in pieces])(*fields)
+    sent = call(
+        functools.partial(pack_kernel, plan), [out(count, 8, LANES) for count in counts for _ in range(parts)]
+    )(*turned, halo)
+    received = [sent[0]] + [xor_swap(sent[m], "tx", m) for m in range(1, parts)]
+    weights = [sent[parts]] + [xor_swap(sent[parts + m], "tx", m) for m in range(1, parts)]
+
     back = -(-3 * NP * cols // parts)
     t = plan.tiles
     shapes = [
@@ -676,12 +705,15 @@
         (t, 2, NODES, LANES),
         (4, t, 3, NODES, LANES),
     ]
-    tables = jnp.asarray(fwd_table), jnp.asarray(adj_table)
-    rough, *kept = call(
-        functools.partial(step_kernel, plan, lift),
-        [out(8, LANES)] + [out(*shape) for shape in shapes],
-        [pltpu.VMEM((t, NODES, LANES), F32), pltpu.VMEM((t, NP, LANES), F32)],
-    )(*received, man, *tables)
+    *kept, zone = call(
+        functools.partial(forward_kernel, plan, lift),
+        [out(*shape) for shape in shapes[:5]] + [out(t, NP, LANES)],
+        [pltpu.VMEM((t, NP, LANES), F32)],
+    )(*received, man, tables[0])
+    rough, final, later = call(
+        functools.partial(adjoint_kernel, plan, lift), [out(8, LANES)] + [out(*shape) for shape in shapes[4:]]
+    )(*weights, man, tables[1], *kept, zone)
+    kept = kept[:4] + [final, later]
     answers = call(
         functools.partial(answer_kernel, plan, lift),
         [out(back + 1, 8, LANES)] * parts,

time: 35.2 us -> 34.9 us (level)
  waiting for transfers between devices: 15.4 us -> 10.2 us
  starting transfers between devices: 12 us -> 16.7 us
    ppermute x9 -> x12, waiting for transfers between devices: 15.4 us -> 10.2 us  [xor_swap(): return lax.ppermute(value, axis, [(i, i ^ bits) for i in range(count)])]
    ppermute x9 -> x12, starting transfers between devices: 12 us -> 16.7 us  [xor_swap(): return lax.ppermute(value, axis, [(i, i ^ bits) for i in range(count)])]
    pallas_call x3 -> x4, Pallas kernels: 3.72 us -> 3.83 us  [the longest x1 1.73 us: local(): call(functools.partial(adjoint_kernel, plan, lift), [out(8, LANES)] + [ou...]
  transfers between devices with their start and end apart: 9 -> 12, of which waited for: 7 -> 9; matrix products, arithmetic and copies ran while one was open for 0% -> 0% of each run, Pallas kernels for 5% -> 10%
where the time goes in v1:
time: 34.9 us; the launch traced here: 34.7 us
  starting transfers between devices  16.7 us (48%)
  waiting for transfers between devices  10.2 us (29%)
  Pallas kernels  6.59 us (19%)
  between operations  0.68 us (2%)
  other arithmetic  0.52 us (1%)
    ppermute x12, starting transfers between devices, xor_swap(): return lax.ppermute(value, axis, [(i, i ^ bits) for i in range(count)])  16.7 us
    ppermute x12, waiting for transfers between devices, xor_swap(): return lax.ppermute(value, axis, [(i, i ^ bits) for i in range(count)])  10.2 us
    pallas_call x1, Pallas kernels, local(): call(functools.partial(adjoint_kernel, plan, lift), [out(8, LANES)] + [ou...  1.73 us
    pallas_call x1, Pallas kernels, local(): call(functools.partial(forward_kernel, plan, lift), [out(*shape) for shap...  1.71 us
    pallas_call x1, Pallas kernels, local(): pl.pallas_call(functools.partial(halo_kernel, cols), out_shape=[jax.Shape...  1.21 us
    pallas_call x1, Pallas kernels, local(): call(functools.partial(finish_kernel, plan), out(3 * NP, NP * cols, rows))  0.89 us
  transfers between devices with their start and end apart: 12, of which 9 were waited for; matrix products, arithmetic and copies ran while one was open for 0% of the time, Pallas kernels for 10%

profile of v1, /device:TPU:0, one launch (start us, length us, event | category | flops | bytes accessed | tf_op | source)
XLA Modules:
  0.0 34.7 jit_solution(18069934194712342054)
XLA Ops:
  0.6 1.2 %shard_map.95 = (f32[8,16,128]{2,1,0:T(8,128)S(1)}, f32[16,16,128]{2,1,0:T(8,128)S(1)}, f32[8,16,128]{2,1,0:T(8,128)S(1)}, s32[1,4,2,128]{3,2,1,0:T(2,128)S(1)},...) custom-call(f32[8,16,128]{2,1,0:T(8,128)} %bitcast.11, ...), custom_call_target="tpu_custom_call" | custom-call | flops 1000000 | bytes 1000000 | tf_op jit(solution)/shard_map/pallas_call | solution.py:677
  1.9 0.6 %collective-permute-start = (f32[5,8,128]{2,1,0:T(8,128)S(1)}, f32[5,8,128]{2,1,0:T(8,128)S(1)}, u32[]{:S(2)}, u32[]{:S(2)}) collective-permute-start(f32[5,8,128]{2,1,0:T(8,128)S(1)} %get-tuple-element.46), channel_id=1, source_target_pairs={{0,2},{2,0},{1,3},{3,1},{4,6},{6,4},{5,7},{7,5},{8,10},{10,8},{9,1... | collective-permute-start | bytes 61448 | tf_op jit(solution)/shard_map/ppermute | solution.py:636
  2.4 0.2 shard_map.96
  2.6 0.6 %collective-permute-done.halo = f32[5,8,128]{2,1,0:T(8,128)S(1)} collective-permute-done((f32[5,8,128]{2,1,0:T(8,128)S(1)}, f32[5,8,128]{2,1,0:T(8,128)S(1)}, u32[]{:S(2)}, u32[]{:S(2)}) %collective-permute-start) | collective-permute-done | bytes 20512 | tf_op jit(solution)/shard_map/ppermute | solution.py:636
  3.3 0.2 shard_map.97
  3.5 3.0 %collective-permute-start.1 = (f32[19,8,128]{2,1,0:T(8,128)S(1)}, f32[19,8,128]{2,1,0:T(8,128)S(1)}, u32[]{:S(2)}, u32[]{:S(2)}) collective-permute-start(f32[19,8,128]{2,1,0:T(8,128)S(1)} %get-tuple-element.48), channel_id=1, source_target_pairs={{0,4},{4,0},{8,12},{12,8},{1,5},{5,1},{9,13},{13,9},{2,6},{6,2},{1... | collective-permute-start | bytes 233480 | tf_op jit(solution)/shard_map/ppermute | solution.py:636
  6.4 2.6 %collective-permute-start.2 = (f32[19,8,128]{2,1,0:T(8,128)S(1)}, f32[19,8,128]{2,1,0:T(8,128)S(1)}, u32[]{:S(2)}, u32[]{:S(2)}) collective-permute-start(f32[19,8,128]{2,1,0:T(8,128)S(1)} %get-tuple-element.49), channel_id=1, source_target_pairs={{0,8},{4,12},{8,0},{12,4},{1,9},{5,13},{9,1},{13,5},{2,10},{6,14},... | collective-permute-start | bytes 233480 | tf_op jit(solution)/shard_map/ppermute | solution.py:636
  9.0 0.0 collective-permute-start.3
  9.0 0.9 %collective-permute-start.4 = (f32[6,8,128]{2,1,0:T(8,128)S(1)}, f32[6,8,128]{2,1,0:T(8,128)S(1)}, u32[]{:S(2)}, u32[]{:S(2)}) collective-permute-start(f32[6,8,128]{2,1,0:T(8,128)S(1)} %get-tuple-element.58), channel_id=1, source_target_pairs={{0,4},{4,0},{8,12},{12,8},{1,5},{5,1},{9,13},{13,9},{2,6},{6,2},{1... | collective-permute-start | bytes 73736 | tf_op jit(solution)/shard_map/ppermute | solution.py:636
  9.9 3.5 %collective-permute-start.5 = (f32[6,8,128]{2,1,0:T(8,128)S(1)}, f32[6,8,128]{2,1,0:T(8,128)S(1)}, u32[]{:S(2)}, u32[]{:S(2)}) collective-permute-start(f32[6,8,128]{2,1,0:T(8,128)S(1)} %get-tuple-element.59), channel_id=1, source_target_pairs={{0,8},{4,12},{8,0},{12,4},{1,9},{5,13},{9,1},{13,5},{2,10},{6,14},... | collective-permute-start | bytes 73736 | tf_op jit(solution)/shard_map/ppermute | solution.py:636
  13.4 0.0 collective-permute-done.1.refs_1_
  13.4 0.3 collective-permute-start.6
  13.7 2.4 %collective-permute-done.2.refs_2_ = f32[19,8,128]{2,1,0:T(8,128)S(1)} collective-permute-done((f32[19,8,128]{2,1,0:T(8,128)S(1)}, f32[19,8,128]{2,1,0:T(8,128)S(1)}, u32[]{:S(2)}, u32[]{:S(2)}) %collective-permute-start.2) | collective-permute-done | bytes 77856 | tf_op jit(solution)/shard_map/ppermute | solution.py:636
  16.1 0.0 collective-permute-done.3.refs_3_
  16.1 1.7 %shard_map.98 = (f32[4,3,3,64,128]{4,3,2,1,0:T(8,128)S(1)}, f32[4,3,8,128]{3,2,1,0:T(8,128)S(1)}, f32[4,3,2,64,128]{4,3,2,1,0:T(8,128)S(1)}, f32[4,3,2,64,128]{4...) custom-call(f32[19,8,128]{2,1,0:T(8,128)S(1)} %get-tuple-element.47.refs_0_, ...), custom_call_target="tpu_custom_call" | custom-call | flops 1000000 | bytes 1000000 | tf_op jit(solution)/shard_map/pallas_call | solution.py:708
  17.8 0.0 collective-permute-done.4.refs_1_
  17.8 0.3 collective-permute-done.5.refs_2_
  18.1 0.9 %collective-permute-done.6.refs_3_ = f32[6,8,128]{2,1,0:T(8,128)S(1)} collective-permute-done((f32[6,8,128]{2,1,0:T(8,128)S(1)}, f32[6,8,128]{2,1,0:T(8,128)S(1)}, u32[]{:S(2)}, u32[]{:S(2)}) %collective-permute-start.6) | collective-permute-done | bytes 24608 | tf_op jit(solution)/shard_map/ppermute | solution.py:636
  19.0 1.7 %shard_map.99 = (f32[8,128]{1,0:T(8,128)S(1)}, f32[3,2,64,128]{3,2,1,0:T(8,128)S(1)}, f32[4,3,3,64,128]{4,3,2,1,0:T(8,128)S(1)}) custom-call(f32[6,8,128]{2,1,0:T(8,128)S(1)} %get-tuple-element.57.refs_0_, f32[6,8,128]{2,1,0:T(8,128)S(1)} %collective-permute-done.4.refs_1_, f32[6,8,128]{2,1,0:T(8,128)S(1)} %collective-permute-done.5.refs_2_, ...), custom_call_target="tpu_custom_call" | custom-call | flops 1000000 | bytes 1000000 | tf_op jit(solution)/shard_map/pallas_call | solution.py:713
  20.8 1.5 %collective-permute-start.7 = (f32[8,128]{1,0:T(8,128)S(1)}, f32[8,128]{1,0:T(8,128)S(1)}, u32[]{:S(2)}, u32[]{:S(2)}) collective-permute-start(f32[8,128]{1,0:T(8,128)S(1)} %get-tuple-element.69.refs_4_), channel_id=1, source_target_pairs={{0,1},{1,0},{2,3},{3,2},{4,5},{5,4},{6,7},{7,6},{8,9},{9,8},{10,11... | collective-permute-start | bytes 12296 | tf_op jit(solution)/shard_map/ppermute | solution.py:636
  22.3 0.7 %shard_map.100 = (f32[13,8,128]{2,1,0:T(8,128)S(1)}, f32[13,8,128]{2,1,0:T(8,128)S(1)}, f32[13,8,128]{2,1,0:T(8,128)S(1)}, f32[13,8,128]{2,1,0:T(8,128)S(1)}) custom-call(bf16[192,256]{1,0:T(8,128)(2,1)S(1)} %get-tuple-element.38.refs_5_.adj_table, f32[4,3,3,64,128]{4,3,2,1,0:T(8,128)S(1)} %get-tuple-element.53.refs_6_.state, ...), custom_call_target="tpu_custom_call" | custom-call | flops 1000000 | bytes 1000000 | tf_op jit(solution)/shard_map/pallas_call | solution.py:717
  22.9 1.5 %collective-permute-done.7.refs_5_ = f32[8,128]{1,0:T(8,128)S(1)} collective-permute-done((f32[8,128]{1,0:T(8,128)S(1)}, f32[8,128]{1,0:T(8,128)S(1)}, u32[]{:S(2)}, u32[]{:S(2)}) %collective-permute-start.7) | collective-permute-done | bytes 4128 | tf_op jit(solution)/shard_map/ppermute | solution.py:636
  24.4 1.1 %collective-permute-start.8 = (f32[13,8,128]{2,1,0:T(8,128)S(1)}, f32[13,8,128]{2,1,0:T(8,128)S(1)}, u32[]{:S(2)}, u32[]{:S(2)}) collective-permute-start(f32[13,8,128]{2,1,0:T(8,128)S(1)} %get-tuple-element.71), channel_id=1, source_target_pairs={{0,4},{4,0},{8,12},{12,8},{1,5},{5,1},{9,13},{13,9},{2,6},{6,2},{1... | collective-permute-start | bytes 159752 | tf_op jit(solution)/shard_map/ppermute | solution.py:636
  25.5 1.6 %collective-permute-start.9 = (f32[13,8,128]{2,1,0:T(8,128)S(1)}, f32[13,8,128]{2,1,0:T(8,128)S(1)}, u32[]{:S(2)}, u32[]{:S(2)}) collective-permute-start(f32[13,8,128]{2,1,0:T(8,128)S(1)} %get-tuple-element.72), channel_id=1, source_target_pairs={{0,8},{4,12},{8,0},{12,4},{1,9},{5,13},{9,1},{13,5},{2,10},{6,14},... | collective-permute-start | bytes 159752 | tf_op jit(solution)/shard_map/ppermute | solution.py:636
  27.1 1.7 %collective-permute-start.10 = (f32[13,8,128]{2,1,0:T(8,128)S(1)}, f32[13,8,128]{2,1,0:T(8,128)S(1)}, u32[]{:S(2)}, u32[]{:S(2)}) collective-permute-start(f32[13,8,128]{2,1,0:T(8,128)S(1)} %get-tuple-element.73), channel_id=1, source_target_pairs={{0,12},{4,8},{8,4},{12,0},{1,13},{5,9},{9,5},{13,1},{2,14},{6,10},... | collective-permute-start | bytes 159752 | tf_op jit(solution)/shard_map/ppermute | solution.py:636
  28.8 0.3 collective-permute-done.8.refs_1_
  29.1 2.0 %collective-permute-done.9.refs_2_ = f32[13,8,128]{2,1,0:T(8,128)S(1)} collective-permute-done((f32[13,8,128]{2,1,0:T(8,128)S(1)}, f32[13,8,128]{2,1,0:T(8,128)S(1)}, u32[]{:S(2)}, u32[]{:S(2)}) %collective-permute-start.9) | collective-permute-done | bytes 53280 | tf_op jit(solution)/shard_map/ppermute | solution.py:636
  31.1 1.9 %collective-permute-done.10.refs_3_ = f32[13,8,128]{2,1,0:T(8,128)S(1)} collective-permute-done((f32[13,8,128]{2,1,0:T(8,128)S(1)}, f32[13,8,128]{2,1,0:T(8,128)S(1)}, u32[]{:S(2)}, u32[]{:S(2)}) %collective-permute-start.10) | collective-permute-done | bytes 53280 | tf_op jit(solution)/shard_map/ppermute | solution.py:636
  33.0 0.0 collective-permute-start.11
  33.0 0.9 %shard_map.102 = f32[24,16,128]{2,1,0:T(8,128)} custom-call(f32[13,8,128]{2,1,0:T(8,128)S(1)} %get-tuple-element.70.refs_0_, f32[13,8,128]{2,1,0:T(8,128)S(1)} %collective-permute-done.8.refs_1_, f32[13,8,128]{2,1,0:T(8,128)S(1)} %collective-permute-done.9.refs_2_, f32[13,8,128]{2,1,0:T(8,128)S(1)} %collective-permute-done.10.refs_3_), custom_call_target="tpu_custom_call" | custom-call | flops 1000000 | bytes 1000000 | tf_op jit(solution)/shard_map/pallas_call | solution.py:742
  33.9 0.3 collective-permute-done.11
  34.2 0.5 %multiply_bitcast_fusion = f32[32]{0:T(128)} fusion(f32[8,128]{1,0:T(8,128)S(1)} %add.21), kind=kLoop, calls=%fused_computation.4 | loop fusion | flops 32 | bytes 256 | tf_op jit(solution)/shard_map/mul | solution.py:745
  (3 shorter events, 0.0 us)
Async XLA Ops:
  1.9 1.4 %collective-permute-start = (f32[5,8,128]{2,1,0:T(8,128)S(1)}, f32[5,8,128]{2,1,0:T(8,128)S(1)}, u32[]{:S(2)}, u32[]{:S(2)}) collective-permute-start(f32[5,8,128]{2,1,0:T(8,128)S(1)} %get-tuple-element.46), channel_id=1, source_target_pairs={{0,2},{2,0},{1,3},{3,1},{4,6},{6,4},{5,7},{7,5},{8,10},{10,8},{9,1... | collective-permute-start | bytes 61448 | tf_op jit(solution)/shard_map/ppermute | solution.py:636
  3.5 10.0 %collective-permute-start.1 = (f32[19,8,128]{2,1,0:T(8,128)S(1)}, f32[19,8,128]{2,1,0:T(8,128)S(1)}, u32[]{:S(2)}, u32[]{:S(2)}) collective-permute-start(f32[19,8,128]{2,1,0:T(8,128)S(1)} %get-tuple-element.48), channel_id=1, source_target_pairs={{0,4},{4,0},{8,12},{12,8},{1,5},{5,1},{9,13},{13,9},{2,6},{6,2},{1... | collective-permute-start | bytes 233480 | tf_op jit(solution)/shard_map/ppermute | solution.py:636
  6.4 9.7 %collective-permute-start.2 = (f32[19,8,128]{2,1,0:T(8,128)S(1)}, f32[19,8,128]{2,1,0:T(8,128)S(1)}, u32[]{:S(2)}, u32[]{:S(2)}) collective-permute-start(f32[19,8,128]{2,1,0:T(8,128)S(1)} %get-tuple-element.49), channel_id=1, source_target_pairs={{0,8},{4,12},{8,0},{12,4},{1,9},{5,13},{9,1},{13,5},{2,10},{6,14},... | collective-permute-start | bytes 233480 | tf_op jit(solution)/shard_map/ppermute | solution.py:636
  9.0 7.1 %collective-permute-start.3 = (f32[19,8,128]{2,1,0:T(8,128)S(1)}, f32[19,8,128]{2,1,0:T(8,128)S(1)}, u32[]{:S(2)}, u32[]{:S(2)}) collective-permute-start(f32[19,8,128]{2,1,0:T(8,128)S(1)} %get-tuple-element.50), channel_id=1, source_target_pairs={{0,12},{4,8},{8,4},{12,0},{1,13},{5,9},{9,5},{13,1},{2,14},{6,10},... | collective-permute-start | bytes 233480 | tf_op jit(solution)/shard_map/ppermute | solution.py:636
  9.0 8.8 %collective-permute-start.4 = (f32[6,8,128]{2,1,0:T(8,128)S(1)}, f32[6,8,128]{2,1,0:T(8,128)S(1)}, u32[]{:S(2)}, u32[]{:S(2)}) collective-permute-start(f32[6,8,128]{2,1,0:T(8,128)S(1)} %get-tuple-element.58), channel_id=1, source_target_pairs={{0,4},{4,0},{8,12},{12,8},{1,5},{5,1},{9,13},{13,9},{2,6},{6,2},{1... | collective-permute-start | bytes 73736 | tf_op jit(solution)/shard_map/ppermute | solution.py:636
  9.9 8.2 %collective-permute-start.5 = (f32[6,8,128]{2,1,0:T(8,128)S(1)}, f32[6,8,128]{2,1,0:T(8,128)S(1)}, u32[]{:S(2)}, u32[]{:S(2)}) collective-permute-start(f32[6,8,128]{2,1,0:T(8,128)S(1)} %get-tuple-element.59), channel_id=1, source_target_pairs={{0,8},{4,12},{8,0},{12,4},{1,9},{5,13},{9,1},{13,5},{2,10},{6,14},... | collective-permute-start | bytes 73736 | tf_op jit(solution)/shard_map/ppermute | solution.py:636
  13.4 5.6 %collective-permute-start.6 = (f32[6,8,128]{2,1,0:T(8,128)S(1)}, f32[6,8,128]{2,1,0:T(8,128)S(1)}, u32[]{:S(2)}, u32[]{:S(2)}) collective-permute-start(f32[6,8,128]{2,1,0:T(8,128)S(1)} %get-tuple-element.60), channel_id=1, source_target_pairs={{0,12},{4,8},{8,4},{12,0},{1,13},{5,9},{9,5},{13,1},{2,14},{6,10},... | collective-permute-start | bytes 73736 | tf_op jit(solution)/shard_map/ppermute | solution.py:636
  20.8 3.6 %collective-permute-start.7 = (f32[8,128]{1,0:T(8,128)S(1)}, f32[8,128]{1,0:T(8,128)S(1)}, u32[]{:S(2)}, u32[]{:S(2)}) collective-permute-start(f32[8,128]{1,0:T(8,128)S(1)} %get-tuple-element.69.refs_4_), channel_id=1, source_target_pairs={{0,1},{1,0},{2,3},{3,2},{4,5},{5,4},{6,7},{7,6},{8,9},{9,8},{10,11... | collective-permute-start | bytes 12296 | tf_op jit(solution)/shard_map/ppermute | solution.py:636
  24.4 4.7 %collective-permute-start.8 = (f32[13,8,128]{2,1,0:T(8,128)S(1)}, f32[13,8,128]{2,1,0:T(8,128)S(1)}, u32[]{:S(2)}, u32[]{:S(2)}) collective-permute-start(f32[13,8,128]{2,1,0:T(8,128)S(1)} %get-tuple-element.71), channel_id=1, source_target_pairs={{0,4},{4,0},{8,12},{12,8},{1,5},{5,1},{9,13},{13,9},{2,6},{6,2},{1... | collective-permute-start | bytes 159752 | tf_op jit(solution)/shard_map/ppermute | solution.py:636
  25.5 5.6 %collective-permute-start.9 = (f32[13,8,128]{2,1,0:T(8,128)S(1)}, f32[13,8,128]{2,1,0:T(8,128)S(1)}, u32[]{:S(2)}, u32[]{:S(2)}) collective-permute-start(f32[13,8,128]{2,1,0:T(8,128)S(1)} %get-tuple-element.72), channel_id=1, source_target_pairs={{0,8},{4,12},{8,0},{12,4},{1,9},{5,13},{9,1},{13,5},{2,10},{6,14},... | collective-permute-start | bytes 159752 | tf_op jit(solution)/shard_map/ppermute | solution.py:636
  27.1 5.9 %collective-permute-start.10 = (f32[13,8,128]{2,1,0:T(8,128)S(1)}, f32[13,8,128]{2,1,0:T(8,128)S(1)}, u32[]{:S(2)}, u32[]{:S(2)}) collective-permute-start(f32[13,8,128]{2,1,0:T(8,128)S(1)} %get-tuple-element.73), channel_id=1, source_target_pairs={{0,12},{4,8},{8,4},{12,0},{1,13},{5,9},{9,5},{13,1},{2,14},{6,10},... | collective-permute-start | bytes 159752 | tf_op jit(solution)/shard_map/ppermute | solution.py:636
  33.0 1.2 %collective-permute-start.11 = (f32[8,128]{1,0:T(8,128)S(1)}, f32[8,128]{1,0:T(8,128)S(1)}, u32[]{:S(2)}, u32[]{:S(2)}) collective-permute-start(f32[8,128]{1,0:T(8,128)S(1)} %fusion.1), channel_id=1, source_target_pairs={{0,2},{2,0},{1,3},{3,1},{4,6},{6,4},{5,7},{7,5},{8,10},{10,8},{9,1... | collective-permute-start | bytes 12296 | tf_op jit(solution)/shard_map/ppermute | solution.py:636
